TPU v7x, 512 devices: a whole 4x4x16 slice. The times are simulated.
512 devices in a mesh: dp: 8 (over y, core), expert: 64 (over x, z).
Axes of the slice: x: 4, y: 4, z: 16, core: 2. Of those that a mesh axis runs over, the one named last changes fastest.
Arguments:
- layer_in: bfloat16 [2048, 4096], P('expert', 'dp'), may hold values from -6 to 6
- grad_out: bfloat16 [2048, 4096], P('expert', 'dp'), may hold values from -6 to 6
- gate_prob: float32 [2048, 8], P('expert'), may hold values from 0.05 to 0.6
- expert_ids: int32 [2048, 8], P('expert'), may hold values from 0 to 31, as said below
- replica_index: int32 [2048, 8], P('expert'), may hold values from 0 to 3, as said below
- slot_expert: int32 [64], replicated, may hold values from 0 to 31, as said below
- w_gate: bfloat16 [64, 4096, 1024], P('expert', None, 'dp')
- w_up: bfloat16 [64, 4096, 1024], P('expert', None, 'dp')
- w_down: bfloat16 [64, 1024, 4096], P('expert', 'dp')
Outputs:
- grad_in: bfloat16 [2048, 4096], P('expert', 'dp')
- grad_w_down: bfloat16 [64, 1024, 4096], P('expert', 'dp')
Inputs may be any that keep to these rules, and one draw needn't show every extreme that they name: `slot_expert`: every expert owns one run of consecutive slots, counted cyclically (slot 63 is followed by slot 0), of 1 to 4 slots; the runs cover all 64 slots. `expert_ids`: the 8 experts of one token are different. `replica_index`: each entry is below the number of slots of the expert of the same choice. Of the 32 tokens of one index of expert, at most 8 choices go to any one slot, and in every draw some slot receives exactly 8 from the tokens of every index of expert.
All inputs are finite; a program needn't handle non-finite values.
Results may differ from a plain program's by a relative error of at most 0.014.
Values may be sent and summed in bfloat16 or wider, within the bound.
No kernel may reach another device: no remote copies, remote signals or barrier semaphores. Data moves between devices by JAX's collectives and lax.ppermute only.
A program may use at most 64 MiB of HBM per device.

v0:
```python
import jax
import jax.numpy as jnp
from jax import lax
from jax.sharding import PartitionSpec as P

TOP = 8


def passed_along(value, axis, steps):
    count = lax.axis_size(axis)
    pairs = [(source, (source + steps) % count) for source in range(count)]
    return lax.ppermute(value, axis, pairs)


def body(
    layer_in, grad_out, gate_prob, expert_ids, replica_index, slot_expert, w_gate, w_up, w_down
):
    slots = lax.axis_size("expert")
    maxrep = min(4, slots // 8)
    tok_count = layer_in.shape[0]
    capacity = tok_count // maxrep
    recv_rows = slots * capacity
    expert_count = (8 - maxrep) * slots // 8
    slot_index = jnp.arange(slots, dtype=jnp.int32)
    expert_index = jnp.arange(expert_count, dtype=jnp.int32)
    is_start = slot_expert != jnp.roll(slot_expert, 1)
    first_slot = jnp.sum(
        jnp.where(
            (slot_expert[None, :] == expert_index[:, None]) & is_start[None, :],
            slot_index[None, :],
            0,
        ),
        axis=1,
    )
    expert_flat = expert_ids.reshape(-1)
    route_slot = jnp.sum(
        jnp.where(expert_flat[:, None] == expert_index[None, :], first_slot[None, :], 0), axis=1
    )
    route_slot = (route_slot + replica_index.reshape(-1)) % slots
    onehot = (route_slot[:, None] == slot_index[None, :]).astype(jnp.int32)
    rank_in_slot = jnp.sum((jnp.cumsum(onehot, axis=0) - onehot) * onehot, axis=1)
    position = route_slot * capacity + rank_in_slot
    prob_flat = gate_prob.reshape(-1)

    def pack(values):
        buffer = jnp.zeros((recv_rows, values.shape[1]), values.dtype).at[position].set(values)
        return buffer.reshape(slots, capacity, values.shape[1])

    repeated = jnp.repeat(grad_out, TOP, axis=0).astype(jnp.float32)
    inputs, scaled = (
        lax.all_gather(
            lax.all_to_all(
                pack(jnp.repeat(layer_in, TOP, axis=0)),
                "expert",
                split_axis=0,
                concat_axis=0,
                tiled=True,
            ),
            "dp",
            axis=2,
            tiled=True,
        ),
        lax.all_gather(
            lax.all_to_all(
                pack((prob_flat[:, None] * repeated).astype(jnp.bfloat16)),
                "expert",
                split_axis=0,
                concat_axis=0,
                tiled=True,
            ),
            "dp",
            axis=2,
            tiled=True,
        ),
    )
    inputs = inputs.reshape(recv_rows, -1)
    scaled = scaled.reshape(recv_rows, -1)
    width = inputs.shape[1]
    gate_matrix = w_gate[0]
    up_matrix = w_up[0]
    down_matrix = w_down[0]
    gate_pre = jnp.dot(inputs, gate_matrix, preferred_element_type=jnp.float32)
    up_pre = jnp.dot(inputs, up_matrix, preferred_element_type=jnp.float32)
    hidden = (jax.nn.silu(gate_pre) * up_pre).astype(jnp.bfloat16)
    contract_last = (((1,), (1,)), ((), ()))
    hidden_grad = lax.dot_general(
        scaled, down_matrix, contract_last, preferred_element_type=jnp.float32
    )
    sigma = jax.nn.sigmoid(gate_pre)
    gate_grad = (hidden_grad * up_pre * sigma * (1.0 + gate_pre * (1.0 - sigma))).astype(
        jnp.bfloat16
    )
    up_grad = (hidden_grad * gate_pre * sigma).astype(jnp.bfloat16)
    partial_value = lax.dot_general(
        gate_grad, gate_matrix, contract_last, preferred_element_type=jnp.float32
    )
    partial_value = partial_value + lax.dot_general(
        up_grad, up_matrix, contract_last, preferred_element_type=jnp.float32
    )
    partial_value = partial_value.reshape(slots, capacity, width)
    summed = lax.psum_scatter(
        partial_value.astype(jnp.bfloat16), "dp", scatter_dimension=2, tiled=True
    ).astype(jnp.float32)
    returned = lax.all_to_all(
        summed.astype(jnp.bfloat16), "expert", split_axis=0, concat_axis=0, tiled=True
    ).astype(summed.dtype)
    flat_back = returned.reshape(recv_rows, -1)
    grad_in = jnp.sum(flat_back[position].reshape(tok_count, TOP, -1), axis=1).astype(jnp.bfloat16)
    slot_partial = lax.dot_general(
        hidden, scaled, (((0,), (0,)), ((), ())), preferred_element_type=jnp.float32
    ).astype(jnp.bfloat16)
    own_index = lax.axis_index("expert")
    expert_here = jnp.sum(jnp.where(slot_index == own_index, slot_expert, 0))

    def same_at(offset):
        neighbour = (own_index - offset) % slots
        match = jnp.any((slot_index == neighbour) & (slot_expert == expert_here))
        return match.astype(jnp.float32)

    total = slot_partial.astype(jnp.float32)
    for distance in range(1, maxrep):
        from_left = passed_along(slot_partial, "expert", distance)
        from_right = passed_along(slot_partial, "expert", -distance)
        total = (
            total
            + same_at(distance) * from_left.astype(jnp.float32)
            + same_at(-distance) * from_right.astype(jnp.float32)
        )
    grad_w_down = total.astype(jnp.bfloat16)[None]
    return (grad_in, grad_w_down)


def solution(mesh):
    placed = (
        P("expert", "dp"),
        P("expert", "dp"),
        P("expert", None),
        P("expert", None),
        P("expert", None),
        P(),
        P("expert", None, "dp"),
        P("expert", None, "dp"),
        P("expert", "dp", None),
    )
    return jax.shard_map(
        body,
        mesh=mesh,
        in_specs=placed,
        out_specs=(P("expert", "dp"), P("expert", "dp", None)),
        check_vma=False,
    )
```

profile of v0, /device:TPU:6, one launch (start us, length us, event | category | flops | bytes accessed | tf_op | source)
XLA Modules:
  0.0 330.9 jit_solution(1470478465016000383)
XLA Ops:
  7.2 0.8 copy.18
  8.1 0.1 reshape.135
  8.2 0.1 reshape.134
  8.3 0.1 reshape.133
  8.4 1.2 slice.14
  9.6 1.3 fusion.38
  10.9 2.1 broadcast_compare_fusion
  13.0 0.8 select_reduce_fusion.1
  13.8 0.8 copy.17
  14.5 0.1 eq.116
  14.6 0.1 select_reduce_fusion
  14.7 0.6 reduce-window.6
  15.4 0.2 slice_reduce_fusion
  15.6 0.1 fusion.30
  15.7 1.9 scatter_custom_fusion.1
  17.6 50.4 %all_to_all.15 = bf16[64,8,512]{2,1,0:T(8,128)(2,1)} all-to-all(bf16[64,8,512]{2,1,0:T(8,128)(2,1)S(1)} %bitcast.69), channel_id=1, replica_groups=mesh['dp'=8,'expert'=64] {'expert'}, dimensions={0} | all-to-all | bytes 1048576 | tf_op jit(solution)/shard_map/all_to_all | solution.py:52
  68.0 0.0 all-gather.3.cloned.1.call-start
  68.1 0.1 copy.22
  68.2 0.1 mul.90
  68.3 1.7 scatter_custom_fusion
  70.0 37.4 %all_to_all.16 = bf16[64,8,512]{2,1,0:T(8,128)(2,1)} all-to-all(bf16[64,8,512]{2,1,0:T(8,128)(2,1)S(1)} %bitcast.70), channel_id=1, replica_groups=mesh['dp'=8,'expert'=64] {'expert'}, dimensions={0} | all-to-all | bytes 1048576 | tf_op jit(solution)/shard_map/all_to_all | solution.py:64
  107.5 3.6 %fusion.1 = f32[512,128]{1,0:T(8,128)S(1)} fusion(bf16[64,8,4096]{2,1,0:T(8,128)(2,1)} %all-gather.5.cloned.1.call-done, bf16[1,4096,128]{2,1,0:T(8,128)(2,1)S(1)} %copy-done), kind=kOutput, calls=%fused_computation.6 | convolution fusion | flops 536870912 | bytes 5505024 | tf_op jit(solution)/shard_map/dot_general | solution.py:82
  111.1 0.1 copy-done.1
  111.2 1.3 fusion.3
  112.4 30.0 %all-gather.3.cloned.1.call-done = bf16[64,8,4096]{2,1,0:T(8,128)(2,1)} async-done(((bf16[64,8,512]{2,1,0:T(8,128)(2,1)}), bf16[64,8,4096]{2,1,0:T(8,128)(2,1)}) %all-gather.3.cloned.1.call-update) | async-done | bytes 4194320 | tf_op jit(solution)/shard_map/all_gather | solution.py:63
  142.5 3.7 %fusion.6 = f32[512,128]{1,0:T(8,128)S(1)} fusion(bf16[64,8,4096]{2,1,0:T(8,128)(2,1)} %all-gather.3.cloned.1.call-done, bf16[1,128,4096]{2,1,0:T(8,128)(2,1)} %param.17), kind=kOutput, calls=%fused_computation.11 | convolution fusion | flops 536870912 | bytes 5505024 | tf_op jit(solution)/shard_map/dot_general | solution.py:86
  146.2 1.3 fusion.8
  147.5 3.2 fusion
  150.7 3.0 convolution_convert_fusion
  153.7 3.6 %collective-permute-start = (bf16[128,4096]{1,0:T(8,128)(2,1)S(1)}, bf16[128,4096]{1,0:T(8,128)(2,1)S(1)}, u32[]{:S(2)}, u32[]{:S(2)}) collective-permute-start(bf16[128,4096]{1,0:T(8,128)(2,1)S(1)} %convolution_convert_fusion), channel_id=1, source_target_pairs={{0,1},{1,2},{2,3},{3,4},{4,5},{5,6},{6,7},{7,8},{8,9},{9,10},{10,1... | collective-permute-start | bytes 3145736 | tf_op jit(solution)/shard_map/ppermute | solution.py:12
  157.3 4.7 %collective-permute-start.1 = (bf16[128,4096]{1,0:T(8,128)(2,1)S(1)}, bf16[128,4096]{1,0:T(8,128)(2,1)}, u32[]{:S(2)}, u32[]{:S(2)}) collective-permute-start(bf16[128,4096]{1,0:T(8,128)(2,1)S(1)} %convolution_convert_fusion), channel_id=1, source_target_pairs={{0,63},{1,0},{2,1},{3,2},{4,3},{5,4},{6,5},{7,6},{8,7},{9,8},{10,9... | collective-permute-start | bytes 3145736 | tf_op jit(solution)/shard_map/ppermute | solution.py:12
  162.0 2.1 collective-permute-start.2
  164.2 6.7 %collective-permute-start.3 = (bf16[128,4096]{1,0:T(8,128)(2,1)S(1)}, bf16[128,4096]{1,0:T(8,128)(2,1)}, u32[]{:S(2)}, u32[]{:S(2)}) collective-permute-start(bf16[128,4096]{1,0:T(8,128)(2,1)S(1)} %convolution_convert_fusion), channel_id=1, source_target_pairs={{0,62},{1,63},{2,0},{3,1},{4,2},{5,3},{6,4},{7,5},{8,6},{9,7},{10,... | collective-permute-start | bytes 3145736 | tf_op jit(solution)/shard_map/ppermute | solution.py:12
  170.9 1.9 collective-permute-start.4
  172.8 11.0 %collective-permute-done = bf16[128,4096]{1,0:T(8,128)(2,1)S(1)} collective-permute-done((bf16[128,4096]{1,0:T(8,128)(2,1)S(1)}, bf16[128,4096]{1,0:T(8,128)(2,1)S(1)}, u32[]{:S(2)}, u32[]{:S(2)}) %collective-permute-start) | collective-permute-done | bytes 1048608 | tf_op jit(solution)/shard_map/ppermute | solution.py:12
  183.9 1.0 copy-done.3
  184.8 5.6 %collective-permute-start.5 = (bf16[128,4096]{1,0:T(8,128)(2,1)S(1)}, bf16[128,4096]{1,0:T(8,128)(2,1)}, u32[]{:S(2)}, u32[]{:S(2)}) collective-permute-start(bf16[128,4096]{1,0:T(8,128)(2,1)S(1)} %convolution_convert_fusion), channel_id=1, source_target_pairs={{0,61},{1,62},{2,63},{3,0},{4,1},{5,2},{6,3},{7,4},{8,5},{9,6},{10... | collective-permute-start | bytes 3145736 | tf_op jit(solution)/shard_map/ppermute | solution.py:12
  190.4 6.6 %reduce-scatter.2.cloned.1.call-done = bf16[64,8,512]{2,1,0:T(8,128)(2,1)} async-done(((bf16[64,8,4096]{2,1,0:T(8,128)(2,1)}), bf16[64,8,512]{2,1,0:T(8,128)(2,1)}) %reduce-scatter.2.cloned.1.call-update) | async-done | bytes 524304 | tf_op jit(solution)/shard_map/reduce_scatter | solution.py:101
  197.0 16.3 %all-to-all-start.2 = ((bf16[64,8,512]{2,1,0:T(8,128)(2,1)}), bf16[64,8,512]{2,1,0:T(8,128)(2,1)S(1)}, u32[]{:S(2)}, u32[]{:S(2)}) async-start(bf16[64,8,512]{2,1,0:T(8,128)(2,1)} %reduce-scatter.2.cloned.1.call-done), calls=%async_computation.3 | async-start | bytes 1048576 | tf_op jit(solution)/shard_map/all_to_all | solution.py:104
  213.4 0.8 and_reduce_fusion.5
  217.9 15.7 %collective-permute-done.3 = bf16[128,4096]{1,0:T(8,128)(2,1)} collective-permute-done((bf16[128,4096]{1,0:T(8,128)(2,1)S(1)}, bf16[128,4096]{1,0:T(8,128)(2,1)}, u32[]{:S(2)}, u32[]{:S(2)}) %collective-permute-start.3) | collective-permute-done | bytes 1048608 | tf_op jit(solution)/shard_map/ppermute | solution.py:12
  233.7 68.4 %collective-permute-done.4 = bf16[128,4096]{1,0:T(8,128)(2,1)} collective-permute-done((bf16[128,4096]{1,0:T(8,128)(2,1)S(1)}, bf16[128,4096]{1,0:T(8,128)(2,1)}, u32[]{:S(2)}, u32[]{:S(2)}) %collective-permute-start.4) | collective-permute-done | bytes 1048608 | tf_op jit(solution)/shard_map/ppermute | solution.py:12
  302.1 3.3 collective-permute-done.5
  305.3 5.1 %fusion.14 = bf16[1,128,4096]{2,1,0:T(8,128)(2,1)} fusion(bf16[128,4096]{1,0:T(8,128)(2,1)} %collective-permute-done.5, f32[]{:T(128)S(6)} %convert_element_type.106, bf16[128,4096]{1,0:T(8,128)(2,1)} %collective-permute-done.4, f32[]{:T(128)S(6)} %convert_element_type.104, bf16[128,4096]{1,0:T(8,128)(2,1)} %collective-permute-done.3, ...), kind=kLoop, calls=%fused_computation.20 | loop fusion | flops 10485760 | bytes 8388632 | tf_op jit(solution)/shard_map/broadcast_in_dim | solution.py:129
  310.5 12.0 %all-to-all-done.2 = bf16[64,8,512]{2,1,0:T(8,128)(2,1)S(1)} async-done(((bf16[64,8,512]{2,1,0:T(8,128)(2,1)}), bf16[64,8,512]{2,1,0:T(8,128)(2,1)S(1)}, u32[]{:S(2)}, u32[]{:S(2)}) %all-to-all-start.2) | async-done | bytes 524320 | tf_op jit(solution)/shard_map/all_to_all | solution.py:104
  322.5 0.1 bitcast_convert_fusion
  322.6 1.0 gather_fusion
  323.6 0.7 bitcast_reduce_fusion
  (26 shorter events, 0.3 us)
Async XLA Ops:
  7.2 100.3 %copy-start = (bf16[1,4096,128]{2,1,0:T(8,128)(2,1)S(1)}, bf16[1,4096,128]{2,1,0:T(8,128)(2,1)}, u32[]{:S(2)}) copy-start(bf16[1,4096,128]{2,1,0:T(8,128)(2,1)} %param.15) | copy-start | bytes 3145732
  7.2 60.9 %copy-start.4 = (bf16[32,512]{1,0:T(8,128)(2,1)S(1)}, bf16[32,512]{1,0:T(8,128)(2,1)}, u32[]{:S(2)}) copy-start(bf16[32,512]{1,0:T(8,128)(2,1)} %param.10) | copy-start | bytes 98308
  7.2 60.9 %copy-start.5 = (f32[32,8]{0,1:T(8,128)S(1)}, f32[32,8]{0,1:T(8,128)}, u32[]{:S(2)}) copy-start(f32[32,8]{0,1:T(8,128)} %param.11) | copy-start | bytes 3076
  7.2 100.3 %all-gather.5.cloned.1.call-start = ((), (), s32[]{:S(2)}) async-start(), calls=%async_computation.5 | async-start | bytes 4718592 | tf_op jit(solution)/shard_map/all_gather | solution.py:51
  68.0 74.5 %all-gather.3.cloned.1.call-start = ((), (), s32[]{:S(2)}) async-start(), calls=%async_computation.4 | async-start | bytes 4718592 | tf_op jit(solution)/shard_map/all_gather | solution.py:63
  107.4 3.7 %copy-start.2 = (bf16[1,4096,128]{2,1,0:T(8,128)(2,1)S(1)}, bf16[1,4096,128]{2,1,0:T(8,128)(2,1)}, u32[]{:S(2)}) copy-start(bf16[1,4096,128]{2,1,0:T(8,128)(2,1)} %param.16) | copy-start | bytes 3145732
  107.4 89.6 %reduce-scatter.2.cloned.1.call-start = ((), (), s32[]{:S(2)}) async-start(), calls=%async_computation.6 | async-start | bytes 4718592 | tf_op jit(solution)/shard_map/reduce_scatter | solution.py:101
  107.5 3.7 %copy-start.1 = (bf16[64,8,4096]{2,1,0:T(8,128)(2,1)S(1)}, bf16[64,8,4096]{2,1,0:T(8,128)(2,1)}, u32[]{:S(2)}) copy-start(bf16[64,8,4096]{2,1,0:T(8,128)(2,1)} %all-gather.5.cloned.1.call-done) | copy-start | bytes 12582916
  153.7 30.2 %collective-permute-start = (bf16[128,4096]{1,0:T(8,128)(2,1)S(1)}, bf16[128,4096]{1,0:T(8,128)(2,1)S(1)}, u32[]{:S(2)}, u32[]{:S(2)}) collective-permute-start(bf16[128,4096]{1,0:T(8,128)(2,1)S(1)} %convolution_convert_fusion), channel_id=1, source_target_pairs={{0,1},{1,2},{2,3},{3,4},{4,5},{5,6},{6,7},{7,8},{8,9},{9,10},{10,1... | collective-permute-start | bytes 3145736 | tf_op jit(solution)/shard_map/ppermute | solution.py:12
  157.3 60.6 %collective-permute-start.1 = (bf16[128,4096]{1,0:T(8,128)(2,1)S(1)}, bf16[128,4096]{1,0:T(8,128)(2,1)}, u32[]{:S(2)}, u32[]{:S(2)}) collective-permute-start(bf16[128,4096]{1,0:T(8,128)(2,1)S(1)} %convolution_convert_fusion), channel_id=1, source_target_pairs={{0,63},{1,0},{2,1},{3,2},{4,3},{5,4},{6,5},{7,6},{8,7},{9,8},{10,9... | collective-permute-start | bytes 3145736 | tf_op jit(solution)/shard_map/ppermute | solution.py:12
  162.0 55.9 %collective-permute-start.2 = (bf16[128,4096]{1,0:T(8,128)(2,1)S(1)}, bf16[128,4096]{1,0:T(8,128)(2,1)}, u32[]{:S(2)}, u32[]{:S(2)}) collective-permute-start(bf16[128,4096]{1,0:T(8,128)(2,1)S(1)} %convolution_convert_fusion), channel_id=1, source_target_pairs={{0,2},{1,3},{2,4},{3,5},{4,6},{5,7},{6,8},{7,9},{8,10},{9,11},{10,... | collective-permute-start | bytes 3145736 | tf_op jit(solution)/shard_map/ppermute | solution.py:12
  164.2 69.5 %collective-permute-start.3 = (bf16[128,4096]{1,0:T(8,128)(2,1)S(1)}, bf16[128,4096]{1,0:T(8,128)(2,1)}, u32[]{:S(2)}, u32[]{:S(2)}) collective-permute-start(bf16[128,4096]{1,0:T(8,128)(2,1)S(1)} %convolution_convert_fusion), channel_id=1, source_target_pairs={{0,62},{1,63},{2,0},{3,1},{4,2},{5,3},{6,4},{7,5},{8,6},{9,7},{10,... | collective-permute-start | bytes 3145736 | tf_op jit(solution)/shard_map/ppermute | solution.py:12
  170.9 131.1 %collective-permute-start.4 = (bf16[128,4096]{1,0:T(8,128)(2,1)S(1)}, bf16[128,4096]{1,0:T(8,128)(2,1)}, u32[]{:S(2)}, u32[]{:S(2)}) collective-permute-start(bf16[128,4096]{1,0:T(8,128)(2,1)S(1)} %convolution_convert_fusion), channel_id=1, source_target_pairs={{0,3},{1,4},{2,5},{3,6},{4,7},{5,8},{6,9},{7,10},{8,11},{9,12},{10... | collective-permute-start | bytes 3145736 | tf_op jit(solution)/shard_map/ppermute | solution.py:12
  183.9 1.0 copy-start.3
  184.8 120.5 %collective-permute-start.5 = (bf16[128,4096]{1,0:T(8,128)(2,1)S(1)}, bf16[128,4096]{1,0:T(8,128)(2,1)}, u32[]{:S(2)}, u32[]{:S(2)}) collective-permute-start(bf16[128,4096]{1,0:T(8,128)(2,1)S(1)} %convolution_convert_fusion), channel_id=1, source_target_pairs={{0,61},{1,62},{2,63},{3,0},{4,1},{5,2},{6,3},{7,4},{8,5},{9,6},{10... | collective-permute-start | bytes 3145736 | tf_op jit(solution)/shard_map/ppermute | solution.py:12
  197.0 125.5 %all-to-all-start.2 = ((bf16[64,8,512]{2,1,0:T(8,128)(2,1)}), bf16[64,8,512]{2,1,0:T(8,128)(2,1)S(1)}, u32[]{:S(2)}, u32[]{:S(2)}) async-start(bf16[64,8,512]{2,1,0:T(8,128)(2,1)} %reduce-scatter.2.cloned.1.call-done), calls=%async_computation.3 | async-start | bytes 1048576 | tf_op jit(solution)/shard_map/all_to_all | solution.py:104
Sparse Core Ops, SparseCore 0:
  68.1 32.3 all-gather.4
  107.5 34.9 all-gather.2
  150.8 46.0 reduce-scatter.1
where the time goes:
time: 337 us; the launch traced here: 331 us
  waiting for transfers between devices  147 us (44%)
  blocking collectives  87.7 us (26%)
  starting transfers between devices  41.1 us (12%)
  between operations  17.9 us (5%)
  matrix products  16 us (5%)
  other arithmetic  13.6 us (4%)
  local copies, waits for them, and re-layouts  7.49 us (2%)
    ppermute x6, waiting for transfers between devices, passed_along(): return lax.ppermute(value, axis, pairs)  98.4 us
    all_to_all x1, blocking collectives, body(): lax.all_to_all(pack(jnp.repeat(layer_in, TOP, axis=0)), 'expert', split_a...  50.4 us
    all_to_all x1, blocking collectives, body(): lax.all_to_all(pack((prob_flat[:, None] * repeated).astype(jnp.bfloat16))...  37.4 us
    all_gather x1, waiting for transfers between devices, body(): lax.all_gather(lax.all_to_all(pack((prob_flat[:, None] * repeated).astype...  30 us
    ppermute x6, starting transfers between devices, passed_along(): return lax.ppermute(value, axis, pairs)  24.7 us
    all_to_all x1, starting transfers between devices, body(): lax.all_to_all(summed.astype(jnp.bfloat16), 'expert', split_axis=0, conca...  16.3 us
    all_to_all x1, waiting for transfers between devices, body(): lax.all_to_all(summed.astype(jnp.bfloat16), 'expert', split_axis=0, conca...  12 us
  transfers between devices with their start and end apart: 10, of which 7 were waited for; matrix products, arithmetic and copies ran while one was open for 5% of the time, Pallas kernels for 0%

commit v1 on v0

--- a/solution.py
+++ b/solution.py
@@ -117,15 +117,12 @@
         match = jnp.any((slot_index == neighbour) & (slot_expert == expert_here))
         return match.astype(jnp.float32)
 
-    total = slot_partial.astype(jnp.float32)
-    for distance in range(1, maxrep):
-        from_left = passed_along(slot_partial, "expert", distance)
-        from_right = passed_along(slot_partial, "expert", -distance)
-        total = (
-            total
-            + same_at(distance) * from_left.astype(jnp.float32)
-            + same_at(-distance) * from_right.astype(jnp.float32)
-        )
+    own = slot_partial.astype(jnp.float32)
+    left = own + same_at(1) * passed_along(slot_partial, "expert", 1).astype(jnp.float32)
+    right = own + same_at(-1) * passed_along(slot_partial, "expert", -1).astype(jnp.float32)
+    far_left = passed_along(left.astype(jnp.bfloat16), "expert", 2).astype(jnp.float32)
+    far_right = passed_along(right.astype(jnp.bfloat16), "expert", -2).astype(jnp.float32)
+    total = left + same_at(2) * far_left + (right - own) + same_at(-2) * far_right
     grad_w_down = total.astype(jnp.bfloat16)[None]
     return (grad_in, grad_w_down)
 

time: 337 us -> 283 us (0.84); the launches traced: 331 us -> 282 us
  waiting for transfers between devices: 147 us -> 105 us
  starting transfers between devices: 41.1 us -> 33.1 us
    ppermute x6 -> x4, waiting for transfers between devices: 98.4 us -> 54.7 us  [passed_along(): return lax.ppermute(value, axis, pairs)]
    all_to_all x1, waiting for transfers between devices: 12 us -> 20.6 us  [body(): lax.all_to_all(summed.astype(jnp.bfloat16), 'expert', split_axis=0, conca...]
    ppermute x6 -> x4, starting transfers between devices: 24.7 us -> 17.2 us  [passed_along(): return lax.ppermute(value, axis, pairs)]
    reduce_scatter x1, waiting for transfers between devices: 6.58 us -> 0.02 us  [body(): lax.psum_scatter(partial_value.astype(jnp.bfloat16), 'dp', scatter_dimens...]
  transfers between devices with their start and end apart: 10 -> 8, of which waited for: 7 -> 6; matrix products, arithmetic and copies ran while one was open for 5% -> 6% of each run, Pallas kernels for 0% -> 0%
where the time goes in v1:
time: 283 us; the launch traced here: 282 us
  waiting for transfers between devices  105 us (37%)
  blocking collectives  87.7 us (31%)
  starting transfers between devices  33.1 us (12%)
  between operations  16.6 us (6%)
  other arithmetic  16.5 us (6%)
  matrix products  16 us (6%)
  local copies, waits for them, and re-layouts  6.52 us (2%)
    ppermute x4, waiting for transfers between devices, passed_along(): return lax.ppermute(value, axis, pairs)  54.7 us
    all_to_all x1, blocking collectives, body(): lax.all_to_all(pack(jnp.repeat(layer_in, TOP, axis=0)), 'expert', split_a...  50.4 us
    all_to_all x1, blocking collectives, body(): lax.all_to_all(pack((prob_flat[:, None] * repeated).astype(jnp.bfloat16))...  37.4 us
    all_gather x1, waiting for transfers between devices, body(): lax.all_gather(lax.all_to_all(pack((prob_flat[:, None] * repeated).astype...  30 us
    all_to_all x1, waiting for transfers between devices, body(): lax.all_to_all(summed.astype(jnp.bfloat16), 'expert', split_axis=0, conca...  20.6 us
    ppermute x4, starting transfers between devices, passed_along(): return lax.ppermute(value, axis, pairs)  17.2 us
    all_to_all x1, starting transfers between devices, body(): lax.all_to_all(summed.astype(jnp.bfloat16), 'expert', split_axis=0, conca...  15.8 us
  transfers between devices with their start and end apart: 8, of which 6 were waited for; matrix products, arithmetic and copies ran while one was open for 6% of the time, Pallas kernels for 0%

profile of v1, /device:TPU:6, one launch (start us, length us, event | category | flops | bytes accessed | tf_op | source)
XLA Modules:
  0.0 281.8 jit_solution(3917994021443419826)
XLA Ops:
  7.2 0.0 all-gather.5.cloned.1.call-start
  7.2 0.8 copy.18
  8.1 0.1 reshape.135
  8.2 0.1 reshape.134
  8.3 0.1 reshape.133
  8.4 1.2 slice.14
  9.6 1.3 fusion.43
  10.9 2.1 broadcast_compare_fusion
  13.0 0.8 select_reduce_fusion.1
  13.8 0.8 copy.17
  14.5 0.1 eq.98
  14.6 0.1 select_reduce_fusion
  14.7 0.6 reduce-window.6
  15.4 0.2 slice_reduce_fusion
  15.6 0.1 fusion.35
  15.7 1.9 scatter_custom_fusion.1
  17.6 50.4 %all_to_all.15 = bf16[64,8,512]{2,1,0:T(8,128)(2,1)} all-to-all(bf16[64,8,512]{2,1,0:T(8,128)(2,1)S(1)} %bitcast.69), channel_id=1, replica_groups=mesh['dp'=8,'expert'=64] {'expert'}, dimensions={0} | all-to-all | bytes 1048576 | tf_op jit(solution)/shard_map/all_to_all | solution.py:52
  68.0 0.0 all-gather.3.cloned.1.call-start
  68.1 0.1 copy.22
  68.2 0.1 mul.78
  68.3 1.7 scatter_custom_fusion
  70.0 37.4 %all_to_all.16 = bf16[64,8,512]{2,1,0:T(8,128)(2,1)} all-to-all(bf16[64,8,512]{2,1,0:T(8,128)(2,1)S(1)} %bitcast.70), channel_id=1, replica_groups=mesh['dp'=8,'expert'=64] {'expert'}, dimensions={0} | all-to-all | bytes 1048576 | tf_op jit(solution)/shard_map/all_to_all | solution.py:64
  107.4 0.0 reduce-scatter.2.cloned.1.call-start
  107.5 3.6 %fusion.1 = f32[512,128]{1,0:T(8,128)S(1)} fusion(bf16[64,8,4096]{2,1,0:T(8,128)(2,1)} %all-gather.5.cloned.1.call-done, bf16[1,4096,128]{2,1,0:T(8,128)(2,1)S(1)} %copy-done), kind=kOutput, calls=%fused_computation.6 | convolution fusion | flops 536870912 | bytes 5505024 | tf_op jit(solution)/shard_map/dot_general | solution.py:82
  111.1 0.1 copy-done.1
  111.2 1.3 fusion.3
  112.4 30.0 %all-gather.3.cloned.1.call-done = bf16[64,8,4096]{2,1,0:T(8,128)(2,1)} async-done(((bf16[64,8,512]{2,1,0:T(8,128)(2,1)}), bf16[64,8,4096]{2,1,0:T(8,128)(2,1)}) %all-gather.3.cloned.1.call-update) | async-done | bytes 4194320 | tf_op jit(solution)/shard_map/all_gather | solution.py:63
  142.5 3.7 %fusion.6 = f32[512,128]{1,0:T(8,128)S(1)} fusion(bf16[64,8,4096]{2,1,0:T(8,128)(2,1)} %all-gather.3.cloned.1.call-done, bf16[1,128,4096]{2,1,0:T(8,128)(2,1)} %param.17), kind=kOutput, calls=%fused_computation.11 | convolution fusion | flops 536870912 | bytes 5505024 | tf_op jit(solution)/shard_map/dot_general | solution.py:86
  146.2 1.3 fusion.13
  147.5 3.2 %fusion = bf16[64,8,4096]{2,1,0:T(8,128)(2,1)} fusion(f32[512,4096]{1,0:T(8,128)S(1)} %fusion.13, bf16[1,4096,128]{2,1,0:T(8,128)(2,1)S(1)} %copy-done.2, f32[512,128]{1,0:T(8,128)S(1)} %fusion.6, f32[512,128]{1,0:T(8,128)S(1)} %fusion.1), kind=kOutput, calls=%fused_computation.4 | convolution fusion | flops 541458432 | bytes 14155776 | tf_op jit(solution)/shard_map/dot_general | solution.py:97
  150.7 3.0 %convolution_convert_fusion = bf16[128,4096]{1,0:T(8,128)(2,1)S(1)} fusion(bf16[64,8,4096]{2,1,0:T(8,128)(2,1)} %all-gather.3.cloned.1.call-done, f32[512,128]{1,0:T(8,128)S(1)} %fusion.3, f32[512,128]{1,0:T(8,128)S(1)} %fusion.1), kind=kOutput, calls=%fused_computation.5 | convolution fusion | flops 537788416 | bytes 5767168 | tf_op jit(solution)/shard_map/dot_general | solution.py:109
  153.7 3.6 %collective-permute-start = (bf16[128,4096]{1,0:T(8,128)(2,1)S(1)}, bf16[128,4096]{1,0:T(8,128)(2,1)S(1)}, u32[]{:S(2)}, u32[]{:S(2)}) collective-permute-start(bf16[128,4096]{1,0:T(8,128)(2,1)S(1)} %convolution_convert_fusion), channel_id=1, source_target_pairs={{0,1},{1,2},{2,3},{3,4},{4,5},{5,6},{6,7},{7,8},{8,9},{9,10},{10,1... | collective-permute-start | bytes 3145736 | tf_op jit(solution)/shard_map/ppermute | solution.py:12
  157.3 4.7 %collective-permute-start.2 = (bf16[128,4096]{1,0:T(8,128)(2,1)S(1)}, bf16[128,4096]{1,0:T(8,128)(2,1)}, u32[]{:S(2)}, u32[]{:S(2)}) collective-permute-start(bf16[128,4096]{1,0:T(8,128)(2,1)S(1)} %convolution_convert_fusion), channel_id=1, source_target_pairs={{0,63},{1,0},{2,1},{3,2},{4,3},{5,4},{6,5},{7,6},{8,7},{9,8},{10,9... | collective-permute-start | bytes 3145736 | tf_op jit(solution)/shard_map/ppermute | solution.py:12
  162.1 0.7 and_reduce_fusion.2
  164.1 19.4 %collective-permute-done = bf16[128,4096]{1,0:T(8,128)(2,1)S(1)} collective-permute-done((bf16[128,4096]{1,0:T(8,128)(2,1)S(1)}, bf16[128,4096]{1,0:T(8,128)(2,1)S(1)}, u32[]{:S(2)}, u32[]{:S(2)}) %collective-permute-start) | collective-permute-done | bytes 1048608 | tf_op jit(solution)/shard_map/ppermute | solution.py:12
  183.5 1.4 collective-permute-done.2
  184.9 3.2 %fusion.12 = (bf16[128,4096]{1,0:T(8,128)(2,1)}, bf16[128,4096]{1,0:T(8,128)(2,1)}) fusion(bf16[128,4096]{1,0:T(8,128)(2,1)S(1)} %collective-permute-done, bf16[128,4096]{1,0:T(8,128)(2,1)S(1)} %convolution_convert_fusion, f32[]{:T(128)S(6)} %convert_element_type.90, bf16[128,4096]{1,0:T(8,128)(2,1)} %collective-permute-done.2, f32[]{:T(128)S(6)} %convert_element_type.95), kind=kLoop, calls=%fused_computation.20 | loop fusion | flops 4718592 | bytes 5242888 | tf_op jit(solution)/shard_map/convert_element_type | solution.py:123
  188.0 5.0 %collective-permute-start.1 = (bf16[128,4096]{1,0:T(8,128)(2,1)}, bf16[128,4096]{1,0:T(8,128)(2,1)}, u32[]{:S(2)}, u32[]{:S(2)}) collective-permute-start(bf16[128,4096]{1,0:T(8,128)(2,1)} %get-tuple-element.6), channel_id=1, source_target_pairs={{0,2},{1,3},{2,4},{3,5},{4,6},{5,7},{6,8},{7,9},{8,10},{9,11},{10,... | collective-permute-start | bytes 3145736 | tf_op jit(solution)/shard_map/ppermute | solution.py:12
  193.0 3.9 %collective-permute-start.3 = (bf16[128,4096]{1,0:T(8,128)(2,1)}, bf16[128,4096]{1,0:T(8,128)(2,1)}, u32[]{:S(2)}, u32[]{:S(2)}) collective-permute-start(bf16[128,4096]{1,0:T(8,128)(2,1)} %get-tuple-element.7), channel_id=1, source_target_pairs={{0,62},{1,63},{2,0},{3,1},{4,2},{5,3},{6,4},{7,5},{8,6},{9,7},{10,... | collective-permute-start | bytes 3145736 | tf_op jit(solution)/shard_map/ppermute | solution.py:12
  196.9 0.0 reduce-scatter.2.cloned.1.call-done
  196.9 15.8 %all-to-all-start.2 = ((bf16[64,8,512]{2,1,0:T(8,128)(2,1)}), bf16[64,8,512]{2,1,0:T(8,128)(2,1)}, u32[]{:S(2)}, u32[]{:S(2)}) async-start(bf16[64,8,512]{2,1,0:T(8,128)(2,1)} %reduce-scatter.2.cloned.1.call-done), calls=%async_computation.3 | async-start | bytes 1048576 | tf_op jit(solution)/shard_map/all_to_all | solution.py:104
  214.1 11.4 %collective-permute-done.1 = bf16[128,4096]{1,0:T(8,128)(2,1)} collective-permute-done((bf16[128,4096]{1,0:T(8,128)(2,1)}, bf16[128,4096]{1,0:T(8,128)(2,1)}, u32[]{:S(2)}, u32[]{:S(2)}) %collective-permute-start.1) | collective-permute-done | bytes 1048608 | tf_op jit(solution)/shard_map/ppermute | solution.py:12
  225.5 22.5 %collective-permute-done.3 = bf16[128,4096]{1,0:T(8,128)(2,1)} collective-permute-done((bf16[128,4096]{1,0:T(8,128)(2,1)}, bf16[128,4096]{1,0:T(8,128)(2,1)}, u32[]{:S(2)}, u32[]{:S(2)}) %collective-permute-start.3) | collective-permute-done | bytes 1048608 | tf_op jit(solution)/shard_map/ppermute | solution.py:12
  248.0 3.9 %fusion.19 = bf16[1,128,4096]{2,1,0:T(8,128)(2,1)} fusion(bf16[128,4096]{1,0:T(8,128)(2,1)} %collective-permute-done.3, f32[]{:T(128)S(6)} %convert_element_type.97, bf16[128,4096]{1,0:T(8,128)(2,1)} %collective-permute-done.2, f32[]{:T(128)S(6)} %convert_element_type.95, bf16[128,4096]{1,0:T(8,128)(2,1)} %collective-permute-done.1, ...), kind=kLoop, calls=%fused_computation.27 | loop fusion | flops 8388608 | bytes 6291472 | tf_op jit(solution)/shard_map/broadcast_in_dim | solution.py:126
  251.9 20.6 %all-to-all-done.2 = bf16[64,8,512]{2,1,0:T(8,128)(2,1)} async-done(((bf16[64,8,512]{2,1,0:T(8,128)(2,1)}), bf16[64,8,512]{2,1,0:T(8,128)(2,1)}, u32[]{:S(2)}, u32[]{:S(2)}) %all-to-all-start.2) | async-done | bytes 524320 | tf_op jit(solution)/shard_map/all_to_all | solution.py:104
  272.4 1.2 bitcast_convert_fusion
  273.6 1.0 gather_fusion
  274.6 0.7 bitcast_reduce_fusion
  (21 shorter events, 0.2 us)
Async XLA Ops:
  7.2 100.3 %copy-start = (bf16[1,4096,128]{2,1,0:T(8,128)(2,1)S(1)}, bf16[1,4096,128]{2,1,0:T(8,128)(2,1)}, u32[]{:S(2)}) copy-start(bf16[1,4096,128]{2,1,0:T(8,128)(2,1)} %param.15) | copy-start | bytes 3145732
  7.2 60.9 %copy-start.3 = (bf16[32,512]{1,0:T(8,128)(2,1)S(1)}, bf16[32,512]{1,0:T(8,128)(2,1)}, u32[]{:S(2)}) copy-start(bf16[32,512]{1,0:T(8,128)(2,1)} %param.10) | copy-start | bytes 98308
  7.2 60.9 %copy-start.4 = (f32[32,8]{0,1:T(8,128)S(1)}, f32[32,8]{0,1:T(8,128)}, u32[]{:S(2)}) copy-start(f32[32,8]{0,1:T(8,128)} %param.11) | copy-start | bytes 3076
  7.2 100.3 %all-gather.5.cloned.1.call-start = ((), (), s32[]{:S(2)}) async-start(), calls=%async_computation.5 | async-start | bytes 4718592 | tf_op jit(solution)/shard_map/all_gather | solution.py:51
  68.0 74.5 %all-gather.3.cloned.1.call-start = ((), (), s32[]{:S(2)}) async-start(), calls=%async_computation.4 | async-start | bytes 4718592 | tf_op jit(solution)/shard_map/all_gather | solution.py:63
  107.4 3.7 %copy-start.2 = (bf16[1,4096,128]{2,1,0:T(8,128)(2,1)S(1)}, bf16[1,4096,128]{2,1,0:T(8,128)(2,1)}, u32[]{:S(2)}) copy-start(bf16[1,4096,128]{2,1,0:T(8,128)(2,1)} %param.16) | copy-start | bytes 3145732
  107.4 89.5 %reduce-scatter.2.cloned.1.call-start = ((), (), s32[]{:S(2)}) async-start(), calls=%async_computation.6 | async-start | bytes 4718592 | tf_op jit(solution)/shard_map/reduce_scatter | solution.py:101
  107.5 3.7 %copy-start.1 = (bf16[64,8,4096]{2,1,0:T(8,128)(2,1)S(1)}, bf16[64,8,4096]{2,1,0:T(8,128)(2,1)}, u32[]{:S(2)}) copy-start(bf16[64,8,4096]{2,1,0:T(8,128)(2,1)} %all-gather.5.cloned.1.call-done) | copy-start | bytes 12582916
  153.7 29.8 %collective-permute-start = (bf16[128,4096]{1,0:T(8,128)(2,1)S(1)}, bf16[128,4096]{1,0:T(8,128)(2,1)S(1)}, u32[]{:S(2)}, u32[]{:S(2)}) collective-permute-start(bf16[128,4096]{1,0:T(8,128)(2,1)S(1)} %convolution_convert_fusion), channel_id=1, source_target_pairs={{0,1},{1,2},{2,3},{3,4},{4,5},{5,6},{6,7},{7,8},{8,9},{9,10},{10,1... | collective-permute-start | bytes 3145736 | tf_op jit(solution)/shard_map/ppermute | solution.py:12
  157.3 27.5 %collective-permute-start.2 = (bf16[128,4096]{1,0:T(8,128)(2,1)S(1)}, bf16[128,4096]{1,0:T(8,128)(2,1)}, u32[]{:S(2)}, u32[]{:S(2)}) collective-permute-start(bf16[128,4096]{1,0:T(8,128)(2,1)S(1)} %convolution_convert_fusion), channel_id=1, source_target_pairs={{0,63},{1,0},{2,1},{3,2},{4,3},{5,4},{6,5},{7,6},{8,7},{9,8},{10,9... | collective-permute-start | bytes 3145736 | tf_op jit(solution)/shard_map/ppermute | solution.py:12
  188.0 37.5 %collective-permute-start.1 = (bf16[128,4096]{1,0:T(8,128)(2,1)}, bf16[128,4096]{1,0:T(8,128)(2,1)}, u32[]{:S(2)}, u32[]{:S(2)}) collective-permute-start(bf16[128,4096]{1,0:T(8,128)(2,1)} %get-tuple-element.6), channel_id=1, source_target_pairs={{0,2},{1,3},{2,4},{3,5},{4,6},{5,7},{6,8},{7,9},{8,10},{9,11},{10,... | collective-permute-start | bytes 3145736 | tf_op jit(solution)/shard_map/ppermute | solution.py:12
  193.0 54.9 %collective-permute-start.3 = (bf16[128,4096]{1,0:T(8,128)(2,1)}, bf16[128,4096]{1,0:T(8,128)(2,1)}, u32[]{:S(2)}, u32[]{:S(2)}) collective-permute-start(bf16[128,4096]{1,0:T(8,128)(2,1)} %get-tuple-element.7), channel_id=1, source_target_pairs={{0,62},{1,63},{2,0},{3,1},{4,2},{5,3},{6,4},{7,5},{8,6},{9,7},{10,... | collective-permute-start | bytes 3145736 | tf_op jit(solution)/shard_map/ppermute | solution.py:12
  196.9 75.5 %all-to-all-start.2 = ((bf16[64,8,512]{2,1,0:T(8,128)(2,1)}), bf16[64,8,512]{2,1,0:T(8,128)(2,1)}, u32[]{:S(2)}, u32[]{:S(2)}) async-start(bf16[64,8,512]{2,1,0:T(8,128)(2,1)} %reduce-scatter.2.cloned.1.call-done), calls=%async_computation.3 | async-start | bytes 1048576 | tf_op jit(solution)/shard_map/all_to_all | solution.py:104
Sparse Core Ops, SparseCore 0:
  68.1 32.3 all-gather.4
  107.5 34.9 all-gather.2
  150.8 45.8 reduce-scatter.1

commit v2 on v1

--- a/solution.py
+++ b/solution.py
@@ -32,49 +32,35 @@
         ),
         axis=1,
     )
-    expert_flat = expert_ids.reshape(-1)
-    route_slot = jnp.sum(
-        jnp.where(expert_flat[:, None] == expert_index[None, :], first_slot[None, :], 0), axis=1
-    )
-    route_slot = (route_slot + replica_index.reshape(-1)) % slots
-    onehot = (route_slot[:, None] == slot_index[None, :]).astype(jnp.int32)
-    rank_in_slot = jnp.sum((jnp.cumsum(onehot, axis=0) - onehot) * onehot, axis=1)
-    position = route_slot * capacity + rank_in_slot
-    prob_flat = gate_prob.reshape(-1)
+    own_index = lax.axis_index("expert")
 
-    def pack(values):
-        buffer = jnp.zeros((recv_rows, values.shape[1]), values.dtype).at[position].set(values)
-        return buffer.reshape(slots, capacity, values.shape[1])
+    def route(ids, replicas):
+        first = jnp.sum(
+            jnp.where(ids[..., None] == expert_index, first_slot, 0), axis=-1
+        )
+        return (first + replicas) % slots
 
-    repeated = jnp.repeat(grad_out, TOP, axis=0).astype(jnp.float32)
-    inputs, scaled = (
-        lax.all_gather(
-            lax.all_to_all(
-                pack(jnp.repeat(layer_in, TOP, axis=0)),
-                "expert",
-                split_axis=0,
-                concat_axis=0,
-                tiled=True,
-            ),
-            "dp",
-            axis=2,
-            tiled=True,
-        ),
-        lax.all_gather(
-            lax.all_to_all(
-                pack((prob_flat[:, None] * repeated).astype(jnp.bfloat16)),
-                "expert",
-                split_axis=0,
-                concat_axis=0,
-                tiled=True,
-            ),
-            "dp",
-            axis=2,
-            tiled=True,
-        ),
-    )
-    inputs = inputs.reshape(recv_rows, -1)
-    scaled = scaled.reshape(recv_rows, -1)
+    codes = (expert_ids * 8 + replica_index).astype(jnp.float32)
+    words = jnp.concatenate([codes, gate_prob], axis=1)
+    all_words = lax.all_gather(words, "expert", axis=0, tiled=True)
+    all_codes = all_words[:, :TOP].astype(jnp.int32)
+    all_prob = all_words[:, TOP:]
+    all_inputs = lax.all_gather(layer_in, "expert", axis=0, tiled=True)
+    all_grads = lax.all_gather(grad_out, "expert", axis=0, tiled=True)
+
+    here = route(all_codes // 8, all_codes % 8) == own_index
+    prob_here = jnp.sum(jnp.where(here, all_prob, 0.0), axis=1)
+    chosen = jnp.any(here, axis=1).astype(jnp.int32).reshape(slots, tok_count)
+    rank = jnp.cumsum(chosen, axis=1) - chosen
+    row = jnp.where(chosen > 0, slot_index[:, None] * capacity + rank, -1).reshape(-1)
+    pick = (jnp.arange(recv_rows, dtype=jnp.int32)[:, None] == row[None, :]).astype(jnp.bfloat16)
+
+    def picked(values):
+        rows = jnp.dot(pick, values, preferred_element_type=jnp.float32).astype(jnp.bfloat16)
+        return lax.all_gather(rows, "dp", axis=1, tiled=True)
+
+    inputs = picked(all_inputs)
+    scaled = picked((prob_here[:, None] * all_grads.astype(jnp.float32)).astype(jnp.bfloat16))
     width = inputs.shape[1]
     gate_matrix = w_gate[0]
     up_matrix = w_up[0]
@@ -100,16 +86,22 @@
     partial_value = partial_value.reshape(slots, capacity, width)
     summed = lax.psum_scatter(
         partial_value.astype(jnp.bfloat16), "dp", scatter_dimension=2, tiled=True
-    ).astype(jnp.float32)
+    )
     returned = lax.all_to_all(
-        summed.astype(jnp.bfloat16), "expert", split_axis=0, concat_axis=0, tiled=True
-    ).astype(summed.dtype)
+        summed, "expert", split_axis=0, concat_axis=0, tiled=True
+    )
     flat_back = returned.reshape(recv_rows, -1)
-    grad_in = jnp.sum(flat_back[position].reshape(tok_count, TOP, -1), axis=1).astype(jnp.bfloat16)
+    route_slot = route(expert_ids, replica_index)
+    onehot = jnp.any(route_slot[:, :, None] == slot_index, axis=1).astype(jnp.int32)
+    rank_back = jnp.cumsum(onehot, axis=0) - onehot
+    place = jnp.arange(capacity, dtype=jnp.int32)
+    unpick = ((onehot[:, :, None] > 0) & (rank_back[:, :, None] == place)).astype(jnp.bfloat16)
+    grad_in = jnp.dot(
+        unpick.reshape(tok_count, recv_rows), flat_back, preferred_element_type=jnp.float32
+    ).astype(jnp.bfloat16)
     slot_partial = lax.dot_general(
         hidden, scaled, (((0,), (0,)), ((), ())), preferred_element_type=jnp.float32
     ).astype(jnp.bfloat16)
-    own_index = lax.axis_index("expert")
     expert_here = jnp.sum(jnp.where(slot_index == own_index, slot_expert, 0))
 
     def same_at(offset):

time: 283 us -> 516 us (1.82)
  waiting for transfers between devices: 105 us -> 319 us
  blocking collectives: 87.7 us -> 106 us
  matrix products: 16 us -> 25.4 us
    all_gather x2 -> x4, waiting for transfers between devices: 30 us -> 243 us  [the longest x1 136 us: body(): all_grads = lax.all_gather(grad_out, 'expert', axis=0, tiled=True)]
    all_gather x0 -> x1, blocking collectives: none -> 106 us  [body(): all_words = lax.all_gather(words, 'expert', axis=0, tiled=True)]
    all_to_all x2 -> x0, blocking collectives: 87.7 us -> none  [the longest x1 50.4 us: body(): lax.all_to_all(pack(jnp.repeat(layer_in, TOP, axis=0)), 'expert', split_a...]
    ppermute x4, waiting for transfers between devices: 54.7 us -> 40.5 us  [passed_along(): return lax.ppermute(value, axis, pairs)]
    all_to_all x1, waiting for transfers between devices: 20.6 us -> 33.4 us  [body(): lax.all_to_all(summed, 'expert', split_axis=0, concat_axis=0, tiled=True)]
    dot_general x0 -> x3, matrix products: none -> 9.36 us  [the longest x2 7.42 us: picked(): jnp.dot(pick, values, preferred_element_type=jnp.float32)]
  transfers between devices with their start and end apart: 8 -> 10, of which waited for: 6 -> 9; matrix products, arithmetic and copies ran while one was open for 6% -> 6% of each run, Pallas kernels for 0% -> 0%
where the time goes in v2:
time: 516 us; the launch traced here: 515 us
  waiting for transfers between devices  319 us (62%)
  blocking collectives  106 us (21%)
  starting transfers between devices  33.2 us (6%)
  matrix products  25.4 us (5%)
  between operations  16.6 us (3%)
  other arithmetic  13 us (3%)
    all_gather x1, waiting for transfers between devices, body(): all_grads = lax.all_gather(grad_out, 'expert', axis=0, tiled=True)  136 us
    all_gather x1, blocking collectives, body(): all_words = lax.all_gather(words, 'expert', axis=0, tiled=True)  106 us
    all_gather x2, waiting for transfers between devices, picked(): return lax.all_gather(rows, 'dp', axis=1, tiled=True)  72.9 us
    ppermute x4, waiting for transfers between devices, passed_along(): return lax.ppermute(value, axis, pairs)  40.5 us
    all_gather x1, waiting for transfers between devices, body(): all_inputs = lax.all_gather(layer_in, 'expert', axis=0, tiled=True)  34.1 us
    all_to_all x1, waiting for transfers between devices, body(): lax.all_to_all(summed, 'expert', split_axis=0, concat_axis=0, tiled=True)  33.4 us
    ppermute x4, starting transfers between devices, passed_along(): return lax.ppermute(value, axis, pairs)  17 us
    all_to_all x1, starting transfers between devices, body(): lax.all_to_all(summed, 'expert', split_axis=0, concat_axis=0, tiled=True)  16 us
  transfers between devices with their start and end apart: 10, of which 9 were waited for; matrix products, arithmetic and copies ran while one was open for 6% of the time, Pallas kernels for 0%

profile of v2, /device:TPU:6, one launch (start us, length us, event | category | flops | bytes accessed | tf_op | source)
XLA Modules:
  0.0 514.9 jit_solution(13106250262551552550)
XLA Ops:
  7.2 0.7 all-gather.10.cloned.1.call-update
  8.0 0.7 all-gather.6.cloned.1.call-update
  8.7 1.2 slice.14
  10.0 0.7 add_convert_fusion.1
  10.7 0.7 maximum_bitcast_fusion
  11.4 106.0 %all-gather = f32[64,32,16]{1,2,0:T(8,128)S(1)} all-gather(f32[1,32,16]{1,2,0:T(8,128)S(1)} %maximum_bitcast_fusion), channel_id=1, replica_groups=mesh['dp'=8,'expert'=64] {'expert'}, dimensions={0}, use_global_device_ids=true | all-gather | bytes 133120 | tf_op jit(solution)/shard_map/all_gather | solution.py:45
  117.3 0.2 copy.26
  117.5 0.2 reshape.58
  117.7 0.6 fusion.42
  118.4 1.4 broadcast_compare_fusion
  119.7 0.1 select_reduce_fusion.2
  119.9 0.4 select_reduce_fusion
  120.4 0.1 fusion.34
  120.5 0.1 reshape.56
  120.6 0.2 reduce_window_sum.25
  120.8 0.1 reduce_window_sum.26
  120.9 0.1 add.91
  120.9 0.1 add.92
  121.0 34.1 %all-gather.10.cloned.1.call-done = bf16[2048,512]{1,0:T(8,128)(2,1)} async-done(((bf16[32,512]{1,0:T(8,128)(2,1)}), bf16[2048,512]{1,0:T(8,128)(2,1)}) %all-gather.10.cloned.1.call-update) | async-done | bytes 2097168 | tf_op jit(solution)/shard_map/all_gather | solution.py:48
  155.1 3.6 fusion.12
  158.8 136.2 %all-gather.6.cloned.1.call-done = bf16[2048,512]{1,0:T(8,128)(2,1)} async-done(((bf16[32,512]{1,0:T(8,128)(2,1)}), bf16[2048,512]{1,0:T(8,128)(2,1)}) %all-gather.6.cloned.1.call-update) | async-done | bytes 2097168 | tf_op jit(solution)/shard_map/all_gather | solution.py:49
  295.1 3.8 fusion.11
  298.9 35.9 %all-gather.12.cloned.1.call-done = bf16[512,4096]{1,0:T(8,128)(2,1)} async-done(((bf16[512,512]{1,0:T(8,128)(2,1)}), bf16[512,4096]{1,0:T(8,128)(2,1)}) %all-gather.12.cloned.1.call-update) | async-done | bytes 4194320 | tf_op jit(solution)/shard_map/all_gather | solution.py:60
  334.9 3.6 fusion.16
  338.5 1.3 fusion.19
  339.7 37.0 %all-gather.8.cloned.1.call-done = bf16[512,4096]{1,0:T(8,128)(2,1)} async-done(((bf16[512,512]{1,0:T(8,128)(2,1)}), bf16[512,4096]{1,0:T(8,128)(2,1)}) %all-gather.8.cloned.1.call-update) | async-done | bytes 4194320 | tf_op jit(solution)/shard_map/all_gather | solution.py:60
  376.7 3.7 fusion.21
  380.4 1.3 fusion.14
  381.7 3.2 fusion
  384.9 3.0 convolution_convert_fusion
  387.9 3.5 collective-permute-start
  391.4 4.7 collective-permute-start.2
  396.1 0.7 and_reduce_fusion.2
  398.2 19.6 %collective-permute-done = bf16[128,4096]{1,0:T(8,128)(2,1)S(1)} collective-permute-done((bf16[128,4096]{1,0:T(8,128)(2,1)S(1)}, bf16[128,4096]{1,0:T(8,128)(2,1)S(1)}, u32[]{:S(2)}, u32[]{:S(2)}) %collective-permute-start) | collective-permute-done | bytes 1048608 | tf_op jit(solution)/shard_map/ppermute | solution.py:12
  417.7 1.2 collective-permute-done.2
  418.9 3.2 fusion.7
  422.1 5.2 %collective-permute-start.1 = (bf16[128,4096]{1,0:T(8,128)(2,1)}, bf16[128,4096]{1,0:T(8,128)(2,1)}, u32[]{:S(2)}, u32[]{:S(2)}) collective-permute-start(bf16[128,4096]{1,0:T(8,128)(2,1)} %get-tuple-element.10), channel_id=1, source_target_pairs={{0,2},{1,3},{2,4},{3,5},{4,6},{5,7},{6,8},{7,9},{8,10},{9,11},{10,... | collective-permute-start | bytes 3145736 | tf_op jit(solution)/shard_map/ppermute | solution.py:12
  427.3 3.7 collective-permute-start.3
  431.0 16.0 %all-to-all-start = ((bf16[64,8,512]{2,1,0:T(8,128)(2,1)}), bf16[64,8,512]{2,1,0:T(8,128)(2,1)}, u32[]{:S(2)}, u32[]{:S(2)}) async-start(bf16[64,8,512]{2,1,0:T(8,128)(2,1)} %reduce-scatter.2.cloned.1.call-done), calls=%async_computation.1 | async-start | bytes 1048576 | tf_op jit(solution)/shard_map/all_to_all | solution.py:90
  447.0 0.1 copy.24
  447.1 0.1 copy.25
  448.5 0.7 select_reduce_fusion.1
  449.2 0.1 fusion.28
  449.4 10.2 %collective-permute-done.1 = bf16[128,4096]{1,0:T(8,128)(2,1)} collective-permute-done((bf16[128,4096]{1,0:T(8,128)(2,1)}, bf16[128,4096]{1,0:T(8,128)(2,1)}, u32[]{:S(2)}, u32[]{:S(2)}) %collective-permute-start.1) | collective-permute-done | bytes 1048608 | tf_op jit(solution)/shard_map/ppermute | solution.py:12
  459.6 9.6 %collective-permute-done.3 = bf16[128,4096]{1,0:T(8,128)(2,1)} collective-permute-done((bf16[128,4096]{1,0:T(8,128)(2,1)}, bf16[128,4096]{1,0:T(8,128)(2,1)}, u32[]{:S(2)}, u32[]{:S(2)}) %collective-permute-start.3) | collective-permute-done | bytes 1048608 | tf_op jit(solution)/shard_map/ppermute | solution.py:12
  469.1 3.9 fusion.23
  473.0 33.4 %all-to-all-done = bf16[64,8,512]{2,1,0:T(8,128)(2,1)} async-done(((bf16[64,8,512]{2,1,0:T(8,128)(2,1)}), bf16[64,8,512]{2,1,0:T(8,128)(2,1)}, u32[]{:S(2)}, u32[]{:S(2)}) %all-to-all-start) | async-done | bytes 524320 | tf_op jit(solution)/shard_map/all_to_all | solution.py:90
  506.4 1.9 fusion.13
  (30 shorter events, 0.5 us)
Async XLA Ops:
  7.2 327.7 %copy-start = (bf16[1,4096,128]{2,1,0:T(8,128)(2,1)S(1)}, bf16[1,4096,128]{2,1,0:T(8,128)(2,1)}, u32[]{:S(2)}) copy-start(bf16[1,4096,128]{2,1,0:T(8,128)(2,1)} %param.15) | copy-start | bytes 3145732
  7.2 110.6 %copy-start.5 = (s32[64]{0:T(128)S(1)}, s32[64]{0:T(128)}, u32[]{:S(2)}) copy-start(s32[64]{0:T(128)} %param.14) | copy-start | bytes 772
  7.2 147.9 %all-gather.10.cloned.1.call-start = ((), (), s32[]{:S(2)}) async-start(), calls=%async_computation.4 | async-start | bytes 2129920 | tf_op jit(solution)/shard_map/all_gather | solution.py:48
  7.9 287.1 %all-gather.6.cloned.1.call-start = ((), (), s32[]{:S(2)}) async-start(), calls=%async_computation.2 | async-start | bytes 2129920 | tf_op jit(solution)/shard_map/all_gather | solution.py:49
  8.7 326.2 %all-gather.12.cloned.1.call-start = ((), (), s32[]{:S(2)}) async-start(), calls=%async_computation.5 | async-start | bytes 4718592 | tf_op jit(solution)/shard_map/all_gather | solution.py:60
  158.8 217.9 %all-gather.8.cloned.1.call-start = ((), (), s32[]{:S(2)}) async-start(), calls=%async_computation.3 | async-start | bytes 4718592 | tf_op jit(solution)/shard_map/all_gather | solution.py:60
  298.9 39.6 %copy-start.2 = (bf16[1,4096,128]{2,1,0:T(8,128)(2,1)S(1)}, bf16[1,4096,128]{2,1,0:T(8,128)(2,1)}, u32[]{:S(2)}) copy-start(bf16[1,4096,128]{2,1,0:T(8,128)(2,1)} %param.16) | copy-start | bytes 3145732
  298.9 132.1 %reduce-scatter.2.cloned.1.call-start = ((), (), s32[]{:S(2)}) async-start(), calls=%async_computation.6 | async-start | bytes 4718592 | tf_op jit(solution)/shard_map/reduce_scatter | solution.py:87
  334.9 3.6 copy-start.1
  387.9 29.8 %collective-permute-start = (bf16[128,4096]{1,0:T(8,128)(2,1)S(1)}, bf16[128,4096]{1,0:T(8,128)(2,1)S(1)}, u32[]{:S(2)}, u32[]{:S(2)}) collective-permute-start(bf16[128,4096]{1,0:T(8,128)(2,1)S(1)} %convolution_convert_fusion), channel_id=1, source_target_pairs={{0,1},{1,2},{2,3},{3,4},{4,5},{5,6},{6,7},{7,8},{8,9},{9,10},{10,1... | collective-permute-start | bytes 3145736 | tf_op jit(solution)/shard_map/ppermute | solution.py:12
  391.4 27.5 %collective-permute-start.2 = (bf16[128,4096]{1,0:T(8,128)(2,1)S(1)}, bf16[128,4096]{1,0:T(8,128)(2,1)}, u32[]{:S(2)}, u32[]{:S(2)}) collective-permute-start(bf16[128,4096]{1,0:T(8,128)(2,1)S(1)} %convolution_convert_fusion), channel_id=1, source_target_pairs={{0,63},{1,0},{2,1},{3,2},{4,3},{5,4},{6,5},{7,6},{8,7},{9,8},{10,9... | collective-permute-start | bytes 3145736 | tf_op jit(solution)/shard_map/ppermute | solution.py:12
  398.1 48.9 %copy-start.3 = (s32[32,8]{0,1:T(8,128)S(1)}, s32[32,8]{0,1:T(8,128)}, u32[]{:S(2)}) copy-start(s32[32,8]{0,1:T(8,128)} %param.12) | copy-start | bytes 3076
  398.2 48.9 %copy-start.4 = (s32[32,8]{0,1:T(8,128)S(1)}, s32[32,8]{0,1:T(8,128)}, u32[]{:S(2)}) copy-start(s32[32,8]{0,1:T(8,128)} %param.13) | copy-start | bytes 3076
  422.1 37.5 %collective-permute-start.1 = (bf16[128,4096]{1,0:T(8,128)(2,1)}, bf16[128,4096]{1,0:T(8,128)(2,1)}, u32[]{:S(2)}, u32[]{:S(2)}) collective-permute-start(bf16[128,4096]{1,0:T(8,128)(2,1)} %get-tuple-element.10), channel_id=1, source_target_pairs={{0,2},{1,3},{2,4},{3,5},{4,6},{5,7},{6,8},{7,9},{8,10},{9,11},{10,... | collective-permute-start | bytes 3145736 | tf_op jit(solution)/shard_map/ppermute | solution.py:12
  427.3 41.9 %collective-permute-start.3 = (bf16[128,4096]{1,0:T(8,128)(2,1)}, bf16[128,4096]{1,0:T(8,128)(2,1)}, u32[]{:S(2)}, u32[]{:S(2)}) collective-permute-start(bf16[128,4096]{1,0:T(8,128)(2,1)} %get-tuple-element.11), channel_id=1, source_target_pairs={{0,62},{1,63},{2,0},{3,1},{4,2},{5,3},{6,4},{7,5},{8,6},{9,7},{10,... | collective-permute-start | bytes 3145736 | tf_op jit(solution)/shard_map/ppermute | solution.py:12
  431.0 75.5 %all-to-all-start = ((bf16[64,8,512]{2,1,0:T(8,128)(2,1)}), bf16[64,8,512]{2,1,0:T(8,128)(2,1)}, u32[]{:S(2)}, u32[]{:S(2)}) async-start(bf16[64,8,512]{2,1,0:T(8,128)(2,1)} %reduce-scatter.2.cloned.1.call-done), calls=%async_computation.1 | async-start | bytes 1048576 | tf_op jit(solution)/shard_map/all_to_all | solution.py:90
Sparse Core Ops, SparseCore 0:
  11.0 144.1 all-gather.9
  158.1 136.9 all-gather.5
  297.8 37.0 all-gather.11
  336.8 39.8 all-gather.7
  385.1 45.8 reduce-scatter.1

commit v3 on v1

--- a/solution.py
+++ b/solution.py
@@ -82,6 +82,10 @@
     gate_pre = jnp.dot(inputs, gate_matrix, preferred_element_type=jnp.float32)
     up_pre = jnp.dot(inputs, up_matrix, preferred_element_type=jnp.float32)
     hidden = (jax.nn.silu(gate_pre) * up_pre).astype(jnp.bfloat16)
+    slot_partial = lax.dot_general(
+        hidden, scaled, (((0,), (0,)), ((), ())), preferred_element_type=jnp.float32
+    ).astype(jnp.bfloat16)
+    slot_partial, scaled = lax.optimization_barrier((slot_partial, scaled))
     contract_last = (((1,), (1,)), ((), ()))
     hidden_grad = lax.dot_general(
         scaled, down_matrix, contract_last, preferred_element_type=jnp.float32
@@ -106,9 +110,6 @@
     ).astype(summed.dtype)
     flat_back = returned.reshape(recv_rows, -1)
     grad_in = jnp.sum(flat_back[position].reshape(tok_count, TOP, -1), axis=1).astype(jnp.bfloat16)
-    slot_partial = lax.dot_general(
-        hidden, scaled, (((0,), (0,)), ((), ())), preferred_element_type=jnp.float32
-    ).astype(jnp.bfloat16)
     own_index = lax.axis_index("expert")
     expert_here = jnp.sum(jnp.where(slot_index == own_index, slot_expert, 0))
 

time: 283 us -> 281 us (level)
    ppermute x4, waiting for transfers between devices: 54.7 us -> 51.1 us  [passed_along(): return lax.ppermute(value, axis, pairs)]
  transfers between devices with their start and end apart: 8 -> 8, of which waited for: 6 -> 7; matrix products, arithmetic and copies ran while one was open for 6% -> 5% of each run, Pallas kernels for 0% -> 0%
where the time goes in v3:
time: 281 us; the launch traced here: 280 us
  waiting for transfers between devices  104 us (37%)
  blocking collectives  87.7 us (31%)
  starting transfers between devices  33.7 us (12%)
  between operations  16.6 us (6%)
  other arithmetic  16.5 us (6%)
  matrix products  14.5 us (5%)
  local copies, waits for them, and re-layouts  7.14 us (3%)
    ppermute x4, waiting for transfers between devices, passed_along(): return lax.ppermute(value, axis, pairs)  51.1 us
    all_to_all x1, blocking collectives, body(): lax.all_to_all(pack(jnp.repeat(layer_in, TOP, axis=0)), 'expert', split_a...  50.4 us
    all_to_all x1, blocking collectives, body(): lax.all_to_all(pack((prob_flat[:, None] * repeated).astype(jnp.bfloat16))...  37.4 us
    all_gather x1, waiting for transfers between devices, body(): lax.all_gather(lax.all_to_all(pack((prob_flat[:, None] * repeated).astype...  29.3 us
    all_to_all x1, waiting for transfers between devices, body(): lax.all_to_all(summed.astype(jnp.bfloat16), 'expert', split_axis=0, conca...  20.8 us
    ppermute x4, starting transfers between devices, passed_along(): return lax.ppermute(value, axis, pairs)  17.2 us
    all_to_all x1, starting transfers between devices, body(): lax.all_to_all(summed.astype(jnp.bfloat16), 'expert', split_axis=0, conca...  16.4 us
  transfers between devices with their start and end apart: 8, of which 7 were waited for; matrix products, arithmetic and copies ran while one was open for 5% of the time, Pallas kernels for 0%

profile of v3, /device:TPU:6, one launch (start us, length us, event | category | flops | bytes accessed | tf_op | source)
XLA Modules:
  0.0 280.3 jit_solution(15586533807323691807)
XLA Ops:
  7.2 0.8 copy.18
  8.1 0.1 reshape.135
  8.2 0.1 reshape.134
  8.3 0.1 reshape.133
  8.4 1.2 slice.14
  9.6 1.3 fusion.41
  10.9 2.1 broadcast_compare_fusion
  13.0 0.8 select_reduce_fusion.1
  13.8 0.8 copy.17
  14.5 0.1 eq.98
  14.6 0.1 select_reduce_fusion
  14.7 0.6 reduce-window.6
  15.4 0.2 slice_reduce_fusion
  15.6 0.1 fusion.33
  15.7 1.9 scatter_custom_fusion
  17.6 50.4 %all_to_all.15 = bf16[64,8,512]{2,1,0:T(8,128)(2,1)} all-to-all(bf16[64,8,512]{2,1,0:T(8,128)(2,1)S(1)} %bitcast.69), channel_id=1, replica_groups=mesh['dp'=8,'expert'=64] {'expert'}, dimensions={0} | all-to-all | bytes 1048576 | tf_op jit(solution)/shard_map/all_to_all | solution.py:52
  68.0 0.0 all-gather.5.cloned.1.call-start
  68.1 0.1 copy.22
  68.2 0.1 mul.80
  68.3 1.7 scatter_custom_fusion.1
  70.0 37.4 %all_to_all.16 = bf16[64,8,512]{2,1,0:T(8,128)(2,1)} all-to-all(bf16[64,8,512]{2,1,0:T(8,128)(2,1)S(1)} %bitcast.70), channel_id=1, replica_groups=mesh['dp'=8,'expert'=64] {'expert'}, dimensions={0} | all-to-all | bytes 1048576 | tf_op jit(solution)/shard_map/all_to_all | solution.py:64
  107.5 3.6 %fusion.3 = f32[512,128]{1,0:T(8,128)S(1)} fusion(bf16[64,8,4096]{2,1,0:T(8,128)(2,1)} %all-gather.3.cloned.1.call-done, bf16[1,4096,128]{2,1,0:T(8,128)(2,1)S(1)} %copy-done), kind=kOutput, calls=%fused_computation.8 | convolution fusion | flops 536870912 | bytes 5505024 | tf_op jit(solution)/shard_map/dot_general | solution.py:82
  111.1 0.1 copy-done.1
  111.2 2.0 fusion.1
  113.1 29.3 %all-gather.5.cloned.1.call-done = bf16[64,8,4096]{2,1,0:T(8,128)(2,1)} async-done(((bf16[64,8,512]{2,1,0:T(8,128)(2,1)}), bf16[64,8,4096]{2,1,0:T(8,128)(2,1)}) %all-gather.5.cloned.1.call-update) | async-done | bytes 4194320 | tf_op jit(solution)/shard_map/all_gather | solution.py:63
  142.5 3.2 %convolution_convert_fusion = bf16[128,4096]{1,0:T(8,128)(2,1)S(1)} fusion(f32[512,128]{1,0:T(8,128)} %fusion.1, f32[512,128]{1,0:T(8,128)S(1)} %fusion.3, bf16[64,8,4096]{2,1,0:T(8,128)(2,1)} %all-gather.5.cloned.1.call-done), kind=kOutput, calls=%fused_computation.5 | convolution fusion | flops 537788416 | bytes 5767168 | tf_op jit(solution)/shard_map/dot_general | solution.py:85
  145.7 0.3 copy-done.2
  146.0 0.3 copy-done.5
  146.3 1.2 fusion.10
  147.6 1.3 fusion.14
  148.8 3.2 %fusion = bf16[64,8,4096]{2,1,0:T(8,128)(2,1)} fusion(f32[512,4096]{1,0:T(8,128)S(1)} %fusion.14, bf16[1,4096,128]{2,1,0:T(8,128)(2,1)S(1)} %copy-done.3, f32[512,128]{1,0:T(8,128)S(1)} %fusion.10, f32[512,128]{1,0:T(8,128)S(1)} %fusion.3), kind=kOutput, calls=%fused_computation.4 | convolution fusion | flops 541458432 | bytes 14155776 | tf_op jit(solution)/shard_map/dot_general | solution.py:101
  152.1 3.6 %collective-permute-start = (bf16[128,4096]{1,0:T(8,128)(2,1)S(1)}, bf16[128,4096]{1,0:T(8,128)(2,1)S(1)}, u32[]{:S(2)}, u32[]{:S(2)}) collective-permute-start(bf16[128,4096]{1,0:T(8,128)(2,1)S(1)} %convolution_convert_fusion), channel_id=1, source_target_pairs={{0,1},{1,2},{2,3},{3,4},{4,5},{5,6},{6,7},{7,8},{8,9},{9,10},{10,1... | collective-permute-start | bytes 3145736 | tf_op jit(solution)/shard_map/ppermute | solution.py:12
  155.7 4.7 %collective-permute-start.2 = (bf16[128,4096]{1,0:T(8,128)(2,1)S(1)}, bf16[128,4096]{1,0:T(8,128)(2,1)}, u32[]{:S(2)}, u32[]{:S(2)}) collective-permute-start(bf16[128,4096]{1,0:T(8,128)(2,1)S(1)} %convolution_convert_fusion), channel_id=1, source_target_pairs={{0,63},{1,0},{2,1},{3,2},{4,3},{5,4},{6,5},{7,6},{8,7},{9,8},{10,9... | collective-permute-start | bytes 3145736 | tf_op jit(solution)/shard_map/ppermute | solution.py:12
  160.5 0.7 and_reduce_fusion.2
  162.5 19.4 %collective-permute-done = bf16[128,4096]{1,0:T(8,128)(2,1)S(1)} collective-permute-done((bf16[128,4096]{1,0:T(8,128)(2,1)S(1)}, bf16[128,4096]{1,0:T(8,128)(2,1)S(1)}, u32[]{:S(2)}, u32[]{:S(2)}) %collective-permute-start) | collective-permute-done | bytes 1048608 | tf_op jit(solution)/shard_map/ppermute | solution.py:12
  181.9 1.4 collective-permute-done.2
  183.2 3.2 %fusion.9 = (bf16[128,4096]{1,0:T(8,128)(2,1)}, bf16[128,4096]{1,0:T(8,128)(2,1)}) fusion(bf16[128,4096]{1,0:T(8,128)(2,1)S(1)} %collective-permute-done, bf16[128,4096]{1,0:T(8,128)(2,1)S(1)} %convolution_convert_fusion, f32[]{:T(128)S(6)} %convert_element_type.90, bf16[128,4096]{1,0:T(8,128)(2,1)} %collective-permute-done.2, f32[]{:T(128)S(6)} %convert_element_type.95), kind=kLoop, calls=%fused_computation.17 | loop fusion | flops 4718592 | bytes 5242888 | tf_op jit(solution)/shard_map/convert_element_type | solution.py:124
  186.4 5.0 %collective-permute-start.1 = (bf16[128,4096]{1,0:T(8,128)(2,1)}, bf16[128,4096]{1,0:T(8,128)(2,1)}, u32[]{:S(2)}, u32[]{:S(2)}) collective-permute-start(bf16[128,4096]{1,0:T(8,128)(2,1)} %get-tuple-element.10), channel_id=1, source_target_pairs={{0,2},{1,3},{2,4},{3,5},{4,6},{5,7},{6,8},{7,9},{8,10},{9,11},{10,... | collective-permute-start | bytes 3145736 | tf_op jit(solution)/shard_map/ppermute | solution.py:12
  191.4 3.9 %collective-permute-start.3 = (bf16[128,4096]{1,0:T(8,128)(2,1)}, bf16[128,4096]{1,0:T(8,128)(2,1)}, u32[]{:S(2)}, u32[]{:S(2)}) collective-permute-start(bf16[128,4096]{1,0:T(8,128)(2,1)} %get-tuple-element.11), channel_id=1, source_target_pairs={{0,62},{1,63},{2,0},{3,1},{4,2},{5,3},{6,4},{7,5},{8,6},{9,7},{10,... | collective-permute-start | bytes 3145736 | tf_op jit(solution)/shard_map/ppermute | solution.py:12
  195.3 2.9 %reduce-scatter.2.cloned.1.call-done = bf16[64,8,512]{2,1,0:T(8,128)(2,1)} async-done(((bf16[64,8,4096]{2,1,0:T(8,128)(2,1)}), bf16[64,8,512]{2,1,0:T(8,128)(2,1)}) %reduce-scatter.2.cloned.1.call-update) | async-done | bytes 524304 | tf_op jit(solution)/shard_map/reduce_scatter | solution.py:105
  198.1 16.4 %all-to-all-start.2 = ((bf16[64,8,512]{2,1,0:T(8,128)(2,1)}), bf16[64,8,512]{2,1,0:T(8,128)(2,1)}, u32[]{:S(2)}, u32[]{:S(2)}) async-start(bf16[64,8,512]{2,1,0:T(8,128)(2,1)} %reduce-scatter.2.cloned.1.call-done), calls=%async_computation.3 | async-start | bytes 1048576 | tf_op jit(solution)/shard_map/all_to_all | solution.py:108
  215.9 7.9 %collective-permute-done.1 = bf16[128,4096]{1,0:T(8,128)(2,1)} collective-permute-done((bf16[128,4096]{1,0:T(8,128)(2,1)}, bf16[128,4096]{1,0:T(8,128)(2,1)}, u32[]{:S(2)}, u32[]{:S(2)}) %collective-permute-start.1) | collective-permute-done | bytes 1048608 | tf_op jit(solution)/shard_map/ppermute | solution.py:12
  223.8 22.4 %collective-permute-done.3 = bf16[128,4096]{1,0:T(8,128)(2,1)} collective-permute-done((bf16[128,4096]{1,0:T(8,128)(2,1)}, bf16[128,4096]{1,0:T(8,128)(2,1)}, u32[]{:S(2)}, u32[]{:S(2)}) %collective-permute-start.3) | collective-permute-done | bytes 1048608 | tf_op jit(solution)/shard_map/ppermute | solution.py:12
  246.2 3.9 %fusion.17 = bf16[1,128,4096]{2,1,0:T(8,128)(2,1)} fusion(bf16[128,4096]{1,0:T(8,128)(2,1)} %collective-permute-done.3, f32[]{:T(128)S(6)} %convert_element_type.97, bf16[128,4096]{1,0:T(8,128)(2,1)} %collective-permute-done.2, f32[]{:T(128)S(6)} %convert_element_type.95, bf16[128,4096]{1,0:T(8,128)(2,1)} %collective-permute-done.1, ...), kind=kLoop, calls=%fused_computation.25 | loop fusion | flops 8388608 | bytes 6291472 | tf_op jit(solution)/shard_map/broadcast_in_dim | solution.py:127
  250.1 20.8 %all-to-all-done.2 = bf16[64,8,512]{2,1,0:T(8,128)(2,1)} async-done(((bf16[64,8,512]{2,1,0:T(8,128)(2,1)}), bf16[64,8,512]{2,1,0:T(8,128)(2,1)}, u32[]{:S(2)}, u32[]{:S(2)}) %all-to-all-start.2) | async-done | bytes 524320 | tf_op jit(solution)/shard_map/all_to_all | solution.py:108
  270.9 1.2 bitcast_convert_fusion
  272.1 1.0 gather_fusion
  273.0 0.7 bitcast_reduce_fusion
  (27 shorter events, 0.3 us)
Async XLA Ops:
  7.2 100.3 %copy-start = (bf16[1,4096,128]{2,1,0:T(8,128)(2,1)S(1)}, bf16[1,4096,128]{2,1,0:T(8,128)(2,1)}, u32[]{:S(2)}) copy-start(bf16[1,4096,128]{2,1,0:T(8,128)(2,1)} %param.15) | copy-start | bytes 3145732
  7.2 60.9 %copy-start.6 = (bf16[32,512]{1,0:T(8,128)(2,1)S(1)}, bf16[32,512]{1,0:T(8,128)(2,1)}, u32[]{:S(2)}) copy-start(bf16[32,512]{1,0:T(8,128)(2,1)} %param.10) | copy-start | bytes 98308
  7.2 60.9 %copy-start.7 = (f32[32,8]{0,1:T(8,128)S(1)}, f32[32,8]{0,1:T(8,128)}, u32[]{:S(2)}) copy-start(f32[32,8]{0,1:T(8,128)} %param.11) | copy-start | bytes 3076
  7.2 100.3 %all-gather.3.cloned.1.call-start = ((), (), s32[]{:S(2)}) async-start(), calls=%async_computation.4 | async-start | bytes 4718592 | tf_op jit(solution)/shard_map/all_gather | solution.py:51
  68.0 74.5 %all-gather.5.cloned.1.call-start = ((), (), s32[]{:S(2)}) async-start(), calls=%async_computation.5 | async-start | bytes 4718592 | tf_op jit(solution)/shard_map/all_gather | solution.py:63
  107.4 3.7 %copy-start.3 = (bf16[1,4096,128]{2,1,0:T(8,128)(2,1)S(1)}, bf16[1,4096,128]{2,1,0:T(8,128)(2,1)}, u32[]{:S(2)}) copy-start(bf16[1,4096,128]{2,1,0:T(8,128)(2,1)} %param.16) | copy-start | bytes 3145732
  107.4 90.7 %reduce-scatter.2.cloned.1.call-start = ((), (), s32[]{:S(2)}) async-start(), calls=%async_computation.6 | async-start | bytes 4718592 | tf_op jit(solution)/shard_map/reduce_scatter | solution.py:105
  107.5 3.7 %copy-start.1 = (bf16[64,8,4096]{2,1,0:T(8,128)(2,1)S(1)}, bf16[64,8,4096]{2,1,0:T(8,128)(2,1)}, u32[]{:S(2)}) copy-start(bf16[64,8,4096]{2,1,0:T(8,128)(2,1)} %all-gather.3.cloned.1.call-done) | copy-start | bytes 12582916
  142.5 3.5 %copy-start.2 = (bf16[64,8,4096]{2,1,0:T(8,128)(2,1)S(1)}, bf16[64,8,4096]{2,1,0:T(8,128)(2,1)}, u32[]{:S(2)}) copy-start(bf16[64,8,4096]{2,1,0:T(8,128)(2,1)} %all-gather.5.cloned.1.call-done) | copy-start | bytes 12582916
  142.5 3.8 %copy-start.5 = (bf16[1,128,4096]{2,1,0:T(8,128)(2,1)S(1)}, bf16[1,128,4096]{2,1,0:T(8,128)(2,1)}, u32[]{:S(2)}) copy-start(bf16[1,128,4096]{2,1,0:T(8,128)(2,1)} %param.17) | copy-start | bytes 3145732
  146.3 1.3 copy-start.4
  152.1 29.8 %collective-permute-start = (bf16[128,4096]{1,0:T(8,128)(2,1)S(1)}, bf16[128,4096]{1,0:T(8,128)(2,1)S(1)}, u32[]{:S(2)}, u32[]{:S(2)}) collective-permute-start(bf16[128,4096]{1,0:T(8,128)(2,1)S(1)} %convolution_convert_fusion), channel_id=1, source_target_pairs={{0,1},{1,2},{2,3},{3,4},{4,5},{5,6},{6,7},{7,8},{8,9},{9,10},{10,1... | collective-permute-start | bytes 3145736 | tf_op jit(solution)/shard_map/ppermute | solution.py:12
  155.7 27.5 %collective-permute-start.2 = (bf16[128,4096]{1,0:T(8,128)(2,1)S(1)}, bf16[128,4096]{1,0:T(8,128)(2,1)}, u32[]{:S(2)}, u32[]{:S(2)}) collective-permute-start(bf16[128,4096]{1,0:T(8,128)(2,1)S(1)} %convolution_convert_fusion), channel_id=1, source_target_pairs={{0,63},{1,0},{2,1},{3,2},{4,3},{5,4},{6,5},{7,6},{8,7},{9,8},{10,9... | collective-permute-start | bytes 3145736 | tf_op jit(solution)/shard_map/ppermute | solution.py:12
  186.4 37.4 %collective-permute-start.1 = (bf16[128,4096]{1,0:T(8,128)(2,1)}, bf16[128,4096]{1,0:T(8,128)(2,1)}, u32[]{:S(2)}, u32[]{:S(2)}) collective-permute-start(bf16[128,4096]{1,0:T(8,128)(2,1)} %get-tuple-element.10), channel_id=1, source_target_pairs={{0,2},{1,3},{2,4},{3,5},{4,6},{5,7},{6,8},{7,9},{8,10},{9,11},{10,... | collective-permute-start | bytes 3145736 | tf_op jit(solution)/shard_map/ppermute | solution.py:12
  191.4 54.8 %collective-permute-start.3 = (bf16[128,4096]{1,0:T(8,128)(2,1)}, bf16[128,4096]{1,0:T(8,128)(2,1)}, u32[]{:S(2)}, u32[]{:S(2)}) collective-permute-start(bf16[128,4096]{1,0:T(8,128)(2,1)} %get-tuple-element.11), channel_id=1, source_target_pairs={{0,62},{1,63},{2,0},{3,1},{4,2},{5,3},{6,4},{7,5},{8,6},{9,7},{10,... | collective-permute-start | bytes 3145736 | tf_op jit(solution)/shard_map/ppermute | solution.py:12
  198.1 72.8 %all-to-all-start.2 = ((bf16[64,8,512]{2,1,0:T(8,128)(2,1)}), bf16[64,8,512]{2,1,0:T(8,128)(2,1)}, u32[]{:S(2)}, u32[]{:S(2)}) async-start(bf16[64,8,512]{2,1,0:T(8,128)(2,1)} %reduce-scatter.2.cloned.1.call-done), calls=%async_computation.3 | async-start | bytes 1048576 | tf_op jit(solution)/shard_map/all_to_all | solution.py:108
Sparse Core Ops, SparseCore 0:
  68.1 32.3 all-gather.2
  107.5 34.9 all-gather.4
  152.2 45.9 reduce-scatter.1
